TPU v7x, 128 devices: a whole 4x4x4 slice. The times are simulated.
128 devices in a mesh: row: 4 (over y), col: 32 (over z, x, core).
Axes of the slice: x: 4, y: 4, z: 4, core: 2. Of those that a mesh axis runs over, the one named last changes fastest.
Arguments:
- tokens: bfloat16 [768, 8192], P('col', 'row'), may hold values from -6 to 6
- gate_weight: bfloat16 [8192, 28672], P('row', 'col'), may hold values from -0.0625 to 0.0625
- up_weight: bfloat16 [8192, 28672], P('row', 'col'), may hold values from -0.0625 to 0.0625
- down_weight: bfloat16 [28672, 8192], P('col', 'row'), may hold values from -0.03125 to 0.03125
- mask_gate: int32 [128, 448], P('row', 'col'), may hold values from 0 to 1, as said below
- mask_up: int32 [128, 448], P('row', 'col'), may hold values from 0 to 1, as said below
- mask_down: int32 [448, 128], P('col', 'row'), may hold values from 0 to 1, as said below
- cotangent: bfloat16 [768, 8192], P('col', 'row'), may hold values from -1.5 to 1.5
Outputs:
- output: bfloat16 [768, 8192], P('col', 'row')
- grad_input: bfloat16 [768, 8192], P('col', 'row')
- grad_gate: bfloat16 [8192, 28672], P('row', 'col')
- grad_up: bfloat16 [8192, 28672], P('row', 'col')
- grad_down: bfloat16 [28672, 8192], P('col', 'row')
Inputs may be any that keep to these rules, and one draw needn't show every extreme that they name: `mask_gate`: 1 where a 64 x 64 block of the weight is kept, 0 where it is pruned. `mask_up`: 1 where a 64 x 64 block of the weight is kept, 0 where it is pruned. `mask_down`: 1 where a 64 x 64 block of the weight is kept, 0 where it is pruned.
All inputs are finite; a program needn't handle non-finite values.
Results may differ from a plain program's by a relative error of at most 0.006.
Values may be sent and summed in bfloat16 or wider, within the bound.
No kernel may reach another device: no remote copies, remote signals or barrier semaphores. Data moves between devices by JAX's collectives and lax.ppermute only.
A program may use at most 128 MiB of HBM per device.

v0:
```python
import jax
import jax.numpy as jnp
from jax import lax
from jax.sharding import PartitionSpec as P

BLOCK = 64


def expand(mask):
    return jnp.repeat(jnp.repeat(mask, BLOCK, 0), BLOCK, 1).astype(jnp.bfloat16)


def contract_last(left, right):
    return lax.dot_general(
        left, right, (((1,), (1,)), ((), ())), preferred_element_type=jnp.float32
    )


def contract_first(left, right):
    return lax.dot_general(
        left, right, (((0,), (0,)), ((), ())), preferred_element_type=jnp.float32
    )


def backward_gates(dhid, gate, up):
    sigma = jax.nn.sigmoid(gate)
    dgate = (dhid * up * sigma * (1.0 + gate * (1.0 - sigma))).astype(jnp.bfloat16)
    dup = (dhid * gate * sigma).astype(jnp.bfloat16)
    return (dgate, dup)


def body(tokens, gate_weight, up_weight, down_weight, mask_gate, mask_up, mask_down, cotangent):
    keep_gate = expand(mask_gate)
    keep_up = expand(mask_up)
    keep_down = expand(mask_down)
    w_gate = gate_weight * keep_gate
    w_up = up_weight * keep_up
    w_down = down_weight * keep_down
    width = w_gate.shape[1]
    panel = lax.all_gather(tokens, "col", axis=0, tiled=True)
    stacked = jnp.concatenate([w_gate, w_up], axis=1)
    partial_both = jnp.dot(panel, stacked, preferred_element_type=jnp.float32)
    summed = lax.psum(partial_both, "row")
    gate = summed[:, :width]
    up = summed[:, width:]
    hidden = (jax.nn.silu(gate) * up).astype(jnp.bfloat16)
    output = lax.psum_scatter(
        jnp.dot(hidden, w_down, preferred_element_type=jnp.float32),
        "col",
        scatter_dimension=0,
        tiled=True,
    ).astype(jnp.bfloat16)
    cot_panel = lax.all_gather(cotangent, "col", axis=0, tiled=True)
    partial_dhid = contract_last(cot_panel, w_down)
    dhid = lax.psum(partial_dhid, "row")
    dgate, dup = backward_gates(dhid, gate, up)
    grad_down = (contract_first(hidden, cot_panel) * keep_down).astype(jnp.bfloat16)
    grad_gate = (contract_first(panel, dgate) * keep_gate).astype(jnp.bfloat16)
    grad_up = (contract_first(panel, dup) * keep_up).astype(jnp.bfloat16)
    grad_input = lax.psum_scatter(
        contract_last(dgate, w_gate) + contract_last(dup, w_up),
        "col",
        scatter_dimension=0,
        tiled=True,
    ).astype(jnp.bfloat16)
    return (output, grad_input, grad_gate, grad_up, grad_down)


def solution(mesh):
    return jax.shard_map(
        body,
        mesh=mesh,
        in_specs=(
            P("col", "row"),
            P("row", "col"),
            P("row", "col"),
            P("col", "row"),
            P("row", "col"),
            P("row", "col"),
            P("col", "row"),
            P("col", "row"),
        ),
        out_specs=(
            P("col", "row"),
            P("col", "row"),
            P("row", "col"),
            P("row", "col"),
            P("col", "row"),
        ),
        check_vma=False,
    )
```

profile of v0, /device:TPU:0, one launch (start us, length us, event | category | flops | bytes accessed | tf_op | source)
XLA Modules:
  0.0 472.1 jit_solution(7040883705480512886)
XLA Ops:
  7.2 0.0 all-gather.5.cloned.1.call-start
  7.2 0.7 all-gather.5.cloned.1.call-update
  7.9 0.0 all-gather.3.cloned.1.call-start
  7.9 0.7 all-gather.3.cloned.1.call-update
  8.6 0.0 all-reduce.3.cloned.1.call-start
  8.7 0.7 convert_element_type.66
  9.4 0.1 broadcast_in_dim.18
  9.5 0.1 convert_element_type.67
  9.7 0.7 convert_element_type.69
  10.4 0.1 broadcast_in_dim.20
  10.5 0.1 convert_element_type.70
  10.7 6.1 %copy.24 = bf16[2048,896]{0,1:T(8,128)(2,1)} copy(bf16[2048,896]{1,0:T(8,128)(2,1)} %param.9) | data formatting | bytes 7340032 | tf_op args[1]
  16.7 0.0 copy-start.5
  16.7 6.1 %copy.25 = bf16[2048,896]{0,1:T(8,128)(2,1)} copy(bf16[2048,896]{1,0:T(8,128)(2,1)} %param.10) | data formatting | bytes 7340032 | tf_op args[2]
  22.8 0.0 copy-done.5
  22.8 0.1 copy.26
  22.9 0.1 broadcast_in_dim.22
  23.0 0.1 convert_element_type.74
  23.2 6.1 %copy.27 = bf16[896,2048]{0,1:T(8,128)(2,1)} copy(bf16[896,2048]{1,0:T(8,128)(2,1)} %param.11) | data formatting | bytes 7340032 | tf_op args[3]
  29.2 0.0 copy-start
  29.2 0.0 copy-start.1
  29.2 4.4 bitcast_multiply_fusion.4
  33.7 0.0 copy-done
  33.7 1.2 copy-done.1
  34.8 3.6 bitcast_multiply_fusion.2
  38.4 19.5 %all-gather.5.cloned.1.call-done = bf16[768,2048]{1,0:T(8,128)(2,1)} async-done(((bf16[24,2048]{1,0:T(8,128)(2,1)}), bf16[768,2048]{1,0:T(8,128)(2,1)}) %all-gather.5.cloned.1.call-update) | async-done | bytes 3145744 | tf_op jit(solution)/shard_map/all_gather | solution.py:53
  57.9 7.6 %convolution_bitcast_fusion = f32[768,896]{0,1:T(8,128)} fusion(bf16[896,2048]{0,1:T(8,128)(2,1)} %bitcast_multiply_fusion.4, bf16[768,2048]{1,0:T(8,128)(2,1)} %all-gather.5.cloned.1.call-done), kind=kOutput, calls=%fused_computation.18 | convolution fusion | flops 2818572288 | bytes 9568256 | tf_op jit(solution)/shard_map/dot_general | solution.py:14
  65.5 39.1 %all-gather.3.cloned.1.call-done = bf16[768,2048]{1,0:T(8,128)(2,1)} async-done(((bf16[24,2048]{1,0:T(8,128)(2,1)}), bf16[768,2048]{1,0:T(8,128)(2,1)}) %all-gather.3.cloned.1.call-update) | async-done | bytes 3145744 | tf_op jit(solution)/shard_map/all_gather | solution.py:40
  104.7 12.3 %fusion.6 = f32[768,1792]{0,1:T(8,128)} fusion(bf16[768,2048]{1,0:T(8,128)(2,1)} %all-gather.3.cloned.1.call-done, bf16[2048,896]{0,1:T(8,128)(2,1)} %get-tuple-element.25, bf16[2048,896]{0,1:T(8,128)(2,1)} %get-tuple-element.26), kind=kOutput, calls=%fused_computation.11 | convolution fusion | flops 5651824640 | bytes 15990784 | tf_op jit(solution)/shard_map/dot_general | solution.py:42
  117.0 0.0 all-reduce.3.cloned.1.call-update
  117.0 0.2 reduce-scatter.5.cloned.1.call-start
  117.3 157.7 %all-reduce.3.cloned.1.call-done = (f32[768,1792]{0,1:T(8,128)}, f32[768,896]{0,1:T(8,128)}) async-done(((f32[768,1792]{0,1:T(8,128)}, f32[768,896]{0,1:T(8,128)}), (f32[768,1792]{0,1:T(8,128)}, f32[768,896]{0,1:T(8,128)})) %all-reduce.3.cloned.1.call-update) | async-done | bytes 8257552 | tf_op jit(solution)/shard_map/psum | solution.py:43
  274.9 0.0 copy-start.3
  274.9 4.3 multiply_convert_fusion.1
  279.2 0.0 copy-start.4
  279.3 0.1 copy-done.3
  279.4 0.0 copy-start.2
  279.4 3.5 fusion.11
  282.9 0.0 copy-done.4
  282.9 0.0 copy-done.2
  283.0 5.4 %convolution_add_fusion = f32[768,2048]{1,0:T(8,128)} fusion(f32[768,2048]{1,0:T(8,128)S(1)} %fusion.11, bf16[768,896]{0,1:T(8,128)(2,1)S(1)} %get-tuple-element.22, bf16[2048,896]{0,1:T(8,128)(2,1)S(1)} %copy-done.2), kind=kOutput, calls=%fused_computation.12 | convolution fusion | flops 2820145152 | bytes 17629184 | tf_op jit(solution)/shard_map/dot_general | solution.py:14
  288.3 0.0 reduce-scatter.5.cloned.1.call-update
  288.4 0.0 reduce-scatter.3.cloned.1.call-start
  288.4 7.4 %fusion.10 = f32[768,2048]{1,0:T(8,128)} fusion(bf16[768,896]{0,1:T(8,128)(2,1)S(1)} %get-tuple-element.24, bf16[896,2048]{0,1:T(8,128)(2,1)} %bitcast_multiply_fusion.4), kind=kOutput, calls=%fused_computation.20 | convolution fusion | flops 2818572288 | bytes 11337728 | tf_op jit(solution)/shard_map/dot_general | solution.py:48
  295.9 0.0 reduce-scatter.3.cloned.1.call-update
  295.9 2.1 broadcast_in_dim.23
  298.0 6.2 %copy.28 = bf16[896,2048]{1,0:T(8,128)(2,1)} copy(bf16[896,2048]{0,1:T(8,128)(2,1)} %bitcast.41) | data formatting | bytes 7340032 | tf_op jit(solution)/shard_map/convert_element_type | solution.py:10
  304.2 7.3 %fusion.5 = bf16[2048,896]{0,1:T(8,128)(2,1)} fusion(bf16[768,896]{0,1:T(8,128)(2,1)} %copy-done.4, bf16[768,2048]{1,0:T(8,128)(2,1)} %all-gather.3.cloned.1.call-done, bf16[2048,14]{0,1:T(8,128)(2,1)S(1)} %convert_element_type.67), kind=kOutput, calls=%fused_computation.7 | convolution fusion | flops 2824077312 | bytes 8249344 | tf_op jit(solution)/shard_map/dot_general | solution.py:20
  311.5 6.2 %copy.29 = bf16[2048,896]{1,0:T(8,128)(2,1)} copy(bf16[2048,896]{0,1:T(8,128)(2,1)} %fusion.5) | data formatting | bytes 7340032
  317.7 6.9 %fusion.4 = bf16[2048,896]{0,1:T(8,128)(2,1)} fusion(bf16[768,896]{0,1:T(8,128)(2,1)S(1)} %get-tuple-element.22, bf16[768,2048]{1,0:T(8,128)(2,1)} %all-gather.3.cloned.1.call-done, bf16[2048,14]{0,1:T(8,128)(2,1)S(1)} %convert_element_type.70), kind=kOutput, calls=%fused_computation.5 | convolution fusion | flops 2824077312 | bytes 8249344 | tf_op jit(solution)/shard_map/dot_general | solution.py:20
  324.6 6.1 %copy.30 = bf16[2048,896]{1,0:T(8,128)(2,1)} copy(bf16[2048,896]{0,1:T(8,128)(2,1)} %fusion.4) | data formatting | bytes 7340032
  330.6 6.9 %multiply_convert_fusion = bf16[896,2048]{1,0:T(8,128)(2,1)} fusion(bf16[896,2048]{1,0:T(8,128)(2,1)} %copy.28, bf16[768,896]{0,1:T(8,128)(2,1)S(1)} %get-tuple-element.24, bf16[768,2048]{1,0:T(8,128)(2,1)} %all-gather.5.cloned.1.call-done), kind=kOutput, calls=%fused_computation.8 | convolution fusion | flops 2824077312 | bytes 11862016 | tf_op jit(solution)/shard_map/dot_general | solution.py:20
  337.5 37.2 %reduce-scatter.5.cloned.1.call-done = f32[24,2048]{1,0:T(8,128)} async-done(((f32[768,2048]{1,0:T(8,128)}), f32[24,2048]{1,0:T(8,128)}) %reduce-scatter.5.cloned.1.call-update) | async-done | bytes 196624 | tf_op jit(solution)/shard_map/reduce_scatter | solution.py:60
  374.8 1.6 convert_element_type.79
  376.3 87.7 %reduce-scatter.3.cloned.1.call-done = f32[24,2048]{1,0:T(8,128)} async-done(((f32[768,2048]{1,0:T(8,128)}), f32[24,2048]{1,0:T(8,128)}) %reduce-scatter.3.cloned.1.call-update) | async-done | bytes 196624 | tf_op jit(solution)/shard_map/reduce_scatter | solution.py:47
  464.0 1.6 convert_element_type.76
  (1 shorter events, 0.0 us)
Async XLA Ops:
  7.2 50.8 %all-gather.5.cloned.1.call-start = ((), (), s32[]{:S(2)}) async-start(), calls=%async_computation.4 | async-start | bytes 3244032 | tf_op jit(solution)/shard_map/all_gather | solution.py:53
  7.9 96.8 %all-gather.3.cloned.1.call-start = ((), (), s32[]{:S(2)}) async-start(), calls=%async_computation.2 | async-start | bytes 3244032 | tf_op jit(solution)/shard_map/all_gather | solution.py:40
  8.6 266.3 %all-reduce.3.cloned.1.call-start = ((), (), s32[]{:S(2)}) async-start(), calls=%async_computation.6 | async-start | bytes 16515072 | tf_op jit(solution)/shard_map/psum | solution.py:43
  16.7 6.1 %copy-start.5 = (s32[14,32]{1,0:T(8,128)S(1)}, s32[14,32]{1,0:T(8,128)}, u32[]{:S(2)}) copy-start(s32[14,32]{1,0:T(8,128)} %param.14) | copy-start | bytes 5380
  29.2 4.4 copy-start
  29.2 5.6 %copy-start.1 = (bf16[2048,896]{0,1:T(8,128)(2,1)S(1)}, bf16[2048,896]{0,1:T(8,128)(2,1)}, u32[]{:S(2)}) copy-start(bf16[2048,896]{0,1:T(8,128)(2,1)} %copy.25) | copy-start | bytes 11010052
  117.0 257.7 %reduce-scatter.5.cloned.1.call-start = ((), (), s32[]{:S(2)}) async-start(), calls=%async_computation.5 | async-start | bytes 6488064 | tf_op jit(solution)/shard_map/reduce_scatter | solution.py:60
  274.9 4.5 copy-start.3
  279.2 3.7 copy-start.4
  279.4 3.5 copy-start.2
  288.4 175.6 %reduce-scatter.3.cloned.1.call-start = ((), (), s32[]{:S(2)}) async-start(), calls=%async_computation.3 | async-start | bytes 6488064 | tf_op jit(solution)/shard_map/reduce_scatter | solution.py:47
Sparse Core Ops, SparseCore 0:
  10.3 47.6 all-gather.4
  60.2 44.4 all-gather.2
  117.2 157.7 all-reduce.2
  288.5 86.2 reduce-scatter.4
  378.3 85.6 reduce-scatter.2
where the time goes:
time: 473 us; the launch traced here: 472 us
  waiting for transfers between devices  343 us (73%)
  matrix products  57.4 us (12%)
  local copies, waits for them, and re-layouts  40.9 us (9%)
  other arithmetic  16.9 us (4%)
  between operations  13.9 us (3%)
    psum x1, waiting for transfers between devices, body(): summed = lax.psum(partial_both, 'row')  158 us
    reduce_scatter x1, waiting for transfers between devices, body(): lax.psum_scatter(jnp.dot(hidden, w_down, preferred_element_type=jnp.float...  87.7 us
    all_gather x1, waiting for transfers between devices, body(): panel = lax.all_gather(tokens, 'col', axis=0, tiled=True)  39.1 us
    reduce_scatter x1, waiting for transfers between devices, body(): lax.psum_scatter(contract_last(dgate, w_gate) + contract_last(dup, w_up),...  37.2 us
    unnamed x17, local copies, waits for them, and re-layouts  31.7 us
    dot_general x3, matrix products, contract_first(): lax.dot_general(left, right, (((0,), (0,)), ((), ())), preferred_element_...  21.1 us
    all_gather x1, waiting for transfers between devices, body(): cot_panel = lax.all_gather(cotangent, 'col', axis=0, tiled=True)  19.5 us
    dot_general x3, matrix products, contract_last(): lax.dot_general(left, right, (((1,), (1,)), ((), ())), preferred_element_...  16.5 us
  transfers between devices with their start and end apart: 5, of which 5 were waited for; matrix products, arithmetic and copies ran while one was open for 18% of the time, Pallas kernels for 0%

commit v1 on v0

--- a/solution.py
+++ b/solution.py
@@ -40,7 +40,7 @@
     panel = lax.all_gather(tokens, "col", axis=0, tiled=True)
     stacked = jnp.concatenate([w_gate, w_up], axis=1)
     partial_both = jnp.dot(panel, stacked, preferred_element_type=jnp.float32)
-    summed = lax.psum(partial_both, "row")
+    summed = jnp.sum(lax.all_gather(partial_both, "row"), axis=0)
     gate = summed[:, :width]
     up = summed[:, width:]
     hidden = (jax.nn.silu(gate) * up).astype(jnp.bfloat16)

time: 473 us -> 576 us (1.22)
  waiting for transfers between devices: 343 us -> 395 us
  local copies, waits for them, and re-layouts: 40.9 us -> 67.7 us
  other arithmetic: 16.9 us -> 39.2 us
    all_gather x0 -> x1, waiting for transfers between devices: none -> 191 us  [body(): summed = jnp.sum(lax.all_gather(partial_both, 'row'), axis=0)]
    psum x1, waiting for transfers between devices: 158 us -> 25.6 us  [body(): dhid = lax.psum(partial_dhid, 'row')]
    all_gather x0 -> x1, local copies, waits for them, and re-layouts: none -> 27.2 us  [body(): summed = jnp.sum(lax.all_gather(partial_both, 'row'), axis=0)]
    reduce_sum x0 -> x1, other arithmetic: none -> 19.3 us  [body(): summed = jnp.sum(lax.all_gather(partial_both, 'row'), axis=0)]
    all_gather x1, waiting for transfers between devices: 39.1 us -> 28.4 us  [body(): panel = lax.all_gather(tokens, 'col', axis=0, tiled=True)]
    unnamed x17 -> x13, local copies, waits for them, and re-layouts: 31.7 us -> 31.2 us
  transfers between devices with their start and end apart: 5 -> 6, of which waited for: 5 -> 6; matrix products, arithmetic and copies ran while one was open for 18% -> 26% of each run, Pallas kernels for 0% -> 0%
where the time goes in v1:
time: 576 us; the launch traced here: 574 us
  waiting for transfers between devices  395 us (69%)
  local copies, waits for them, and re-layouts  67.7 us (12%)
  matrix products  57.5 us (10%)
  other arithmetic  39.2 us (7%)
  between operations  14.2 us (2%)
    all_gather x1, waiting for transfers between devices, body(): summed = jnp.sum(lax.all_gather(partial_both, 'row'), axis=0)  191 us
    reduce_scatter x1, waiting for transfers between devices, body(): lax.psum_scatter(jnp.dot(hidden, w_down, preferred_element_type=jnp.float...  88.1 us
    reduce_scatter x1, waiting for transfers between devices, body(): lax.psum_scatter(contract_last(dgate, w_gate) + contract_last(dup, w_up),...  36.8 us
    unnamed x13, local copies, waits for them, and re-layouts  31.2 us
    all_gather x1, waiting for transfers between devices, body(): panel = lax.all_gather(tokens, 'col', axis=0, tiled=True)  28.4 us
    all_gather x1, local copies, waits for them, and re-layouts, body(): summed = jnp.sum(lax.all_gather(partial_both, 'row'), axis=0)  27.2 us
    psum x1, waiting for transfers between devices, body(): dhid = lax.psum(partial_dhid, 'row')  25.6 us
    all_gather x1, waiting for transfers between devices, body(): cot_panel = lax.all_gather(cotangent, 'col', axis=0, tiled=True)  22.9 us
  transfers between devices with their start and end apart: 6, of which 6 were waited for; matrix products, arithmetic and copies ran while one was open for 26% of the time, Pallas kernels for 0%

profile of v1, /device:TPU:0, one launch (start us, length us, event | category | flops | bytes accessed | tf_op | source)
XLA Modules:
  0.0 573.8 jit_solution(14474079112695014374)
XLA Ops:
  7.2 0.0 all-gather.5.cloned.1.call-start
  7.2 0.7 all-gather.5.cloned.1.call-update
  7.9 0.0 all-gather.7.cloned.1.call-start
  7.9 0.7 all-gather.7.cloned.1.call-update
  8.6 0.0 all-gather.9.cloned.1.call-start
  8.7 0.7 convert_element_type.66
  9.4 0.1 broadcast_in_dim.18
  9.5 0.1 convert_element_type.67
  9.7 0.7 convert_element_type.69
  10.4 0.1 broadcast_in_dim.20
  10.5 0.1 convert_element_type.70
  10.7 6.1 %copy.24 = bf16[2048,896]{0,1:T(8,128)(2,1)} copy(bf16[2048,896]{1,0:T(8,128)(2,1)} %param.9) | data formatting | bytes 7340032 | tf_op args[1]
  16.7 6.0 %copy.25 = bf16[2048,896]{0,1:T(8,128)(2,1)} copy(bf16[2048,896]{1,0:T(8,128)(2,1)} %param.10) | data formatting | bytes 7340032 | tf_op args[2]
  22.8 6.8 %bitcast_multiply_fusion.2 = (bf16[2048,896]{0,1:T(8,128)(2,1)}, bf16[2048,896]{0,1:T(8,128)(2,1)}) fusion(bf16[2048,896]{0,1:T(8,128)(2,1)} %copy.25, bf16[2048,14]{0,1:T(8,128)(2,1)S(1)} %convert_element_type.70, bf16[2048,896]{0,1:T(8,128)(2,1)} %copy.24, bf16[2048,14]{0,1:T(8,128)(2,1)S(1)} %convert_element_type.67), kind=kLoop, calls=%fused_computation.9 | loop fusion | flops 3670016 | bytes 14794752 | tf_op jit(solution)/shard_map/mul | solution.py:37
  29.6 28.4 %all-gather.5.cloned.1.call-done = bf16[768,2048]{1,0:T(8,128)(2,1)} async-done(((bf16[24,2048]{1,0:T(8,128)(2,1)}), bf16[768,2048]{1,0:T(8,128)(2,1)}) %all-gather.5.cloned.1.call-update) | async-done | bytes 3145744 | tf_op jit(solution)/shard_map/all_gather | solution.py:40
  57.9 12.4 %fusion.6 = f32[768,1792]{0,1:T(8,128)} fusion(bf16[768,2048]{1,0:T(8,128)(2,1)} %all-gather.5.cloned.1.call-done, bf16[2048,896]{0,1:T(8,128)(2,1)} %get-tuple-element.23, bf16[2048,896]{0,1:T(8,128)(2,1)} %get-tuple-element.24), kind=kOutput, calls=%fused_computation.11 | convolution fusion | flops 5651824640 | bytes 15990784 | tf_op jit(solution)/shard_map/dot_general | solution.py:42
  70.4 0.0 copy-start.3
  70.4 0.0 all-gather.9.cloned.1.call-update
  70.4 0.0 all-reduce.2.cloned.1.call-start
  70.4 0.6 copy-done.3
  71.1 0.1 copy.26
  71.2 0.1 broadcast_in_dim.22
  71.3 0.1 convert_element_type.74
  71.4 6.1 %copy.27 = bf16[896,2048]{0,1:T(8,128)(2,1)} copy(bf16[896,2048]{1,0:T(8,128)(2,1)} %param.11) | data formatting | bytes 7340032 | tf_op args[3]
  77.5 4.2 bitcast_multiply_fusion.4
  81.7 22.9 %all-gather.7.cloned.1.call-done = bf16[768,2048]{1,0:T(8,128)(2,1)} async-done(((bf16[24,2048]{1,0:T(8,128)(2,1)}), bf16[768,2048]{1,0:T(8,128)(2,1)}) %all-gather.7.cloned.1.call-update) | async-done | bytes 3145744 | tf_op jit(solution)/shard_map/all_gather | solution.py:53
  104.7 7.6 %convolution_bitcast_fusion = f32[768,896]{0,1:T(8,128)} fusion(bf16[896,2048]{0,1:T(8,128)(2,1)} %bitcast_multiply_fusion.4, bf16[768,2048]{1,0:T(8,128)(2,1)} %all-gather.7.cloned.1.call-done), kind=kOutput, calls=%fused_computation.18 | convolution fusion | flops 2818572288 | bytes 9568256 | tf_op jit(solution)/shard_map/dot_general | solution.py:14
  112.3 0.0 all-reduce.2.cloned.1.call-update
  112.3 0.2 reduce-scatter.5.cloned.1.call-start
  112.5 191.3 %all-gather.9.cloned.1.call-done = f32[3072,1792]{0,1:T(8,128)} async-done(((f32[768,1792]{0,1:T(8,128)}), f32[3072,1792]{0,1:T(8,128)}) %all-gather.9.cloned.1.call-update) | async-done | bytes 22020112 | tf_op jit(solution)/shard_map/all_gather | solution.py:43
  303.8 27.2 %reshape.22 = f32[4,768,1792]{1,0,2:T(4,128)} reshape(f32[3072,1792]{0,1:T(8,128)} %all-gather.9.cloned.1.call-done) | data formatting | bytes 44040192 | tf_op jit(solution)/shard_map/all_gather | solution.py:43
  331.0 19.3 %reduce_sum.9 = f32[768,1792]{0,1:T(8,128)} reduce(f32[4,768,1792]{1,0,2:T(4,128)} %reshape.22, f32[]{:T(128)} %constant.2.clone.1), dimensions={0}, to_apply=%region_0.0 | reduce | flops 4128768 | bytes 27525124 | tf_op jit(solution)/shard_map/reduce_sum | solution.py:43
  350.3 25.6 %all-reduce.2.cloned.1.call-done = f32[768,896]{0,1:T(8,128)} async-done(((f32[768,896]{0,1:T(8,128)}), f32[768,896]{0,1:T(8,128)}) %all-reduce.2.cloned.1.call-update) | async-done | bytes 2752528 | tf_op jit(solution)/shard_map/psum | solution.py:55
  375.9 0.0 copy-start.1
  375.9 4.3 multiply_convert_fusion.1
  380.2 0.0 copy-start.2
  380.2 0.1 copy-done.1
  380.3 0.0 copy-start
  380.3 3.5 fusion.11
  383.9 0.0 copy-done.2
  383.9 0.0 copy-done
  383.9 5.4 convolution_add_fusion
  389.3 0.0 reduce-scatter.5.cloned.1.call-update
  389.3 0.3 reduce-scatter.3.cloned.1.call-start
  389.6 7.5 %fusion.10 = f32[768,2048]{1,0:T(8,128)} fusion(bf16[768,896]{0,1:T(8,128)(2,1)S(1)} %get-tuple-element.22, bf16[896,2048]{0,1:T(8,128)(2,1)} %bitcast_multiply_fusion.4), kind=kOutput, calls=%fused_computation.20 | convolution fusion | flops 2818572288 | bytes 11337728 | tf_op jit(solution)/shard_map/dot_general | solution.py:48
  397.1 0.0 reduce-scatter.3.cloned.1.call-update
  397.1 2.1 broadcast_in_dim.23
  399.2 6.3 %copy.28 = bf16[896,2048]{1,0:T(8,128)(2,1)} copy(bf16[896,2048]{0,1:T(8,128)(2,1)} %bitcast.43) | data formatting | bytes 7340032 | tf_op jit(solution)/shard_map/convert_element_type | solution.py:10
  405.5 7.3 %fusion.5 = bf16[2048,896]{0,1:T(8,128)(2,1)} fusion(bf16[768,896]{0,1:T(8,128)(2,1)} %copy-done.2, bf16[768,2048]{1,0:T(8,128)(2,1)} %all-gather.5.cloned.1.call-done, bf16[2048,14]{0,1:T(8,128)(2,1)S(1)} %convert_element_type.67), kind=kOutput, calls=%fused_computation.7 | convolution fusion | flops 2824077312 | bytes 8249344 | tf_op jit(solution)/shard_map/dot_general | solution.py:20
  412.8 6.2 %copy.29 = bf16[2048,896]{1,0:T(8,128)(2,1)} copy(bf16[2048,896]{0,1:T(8,128)(2,1)} %fusion.5) | data formatting | bytes 7340032
  419.0 6.9 %fusion.4 = bf16[2048,896]{0,1:T(8,128)(2,1)} fusion(bf16[768,896]{0,1:T(8,128)(2,1)S(1)} %get-tuple-element.20, bf16[768,2048]{1,0:T(8,128)(2,1)} %all-gather.5.cloned.1.call-done, bf16[2048,14]{0,1:T(8,128)(2,1)S(1)} %convert_element_type.70), kind=kOutput, calls=%fused_computation.5 | convolution fusion | flops 2824077312 | bytes 8249344 | tf_op jit(solution)/shard_map/dot_general | solution.py:20
  425.9 6.1 %copy.30 = bf16[2048,896]{1,0:T(8,128)(2,1)} copy(bf16[2048,896]{0,1:T(8,128)(2,1)} %fusion.4) | data formatting | bytes 7340032
  432.0 6.9 %multiply_convert_fusion = bf16[896,2048]{1,0:T(8,128)(2,1)} fusion(bf16[896,2048]{1,0:T(8,128)(2,1)} %copy.28, bf16[768,896]{0,1:T(8,128)(2,1)S(1)} %get-tuple-element.22, bf16[768,2048]{1,0:T(8,128)(2,1)} %all-gather.7.cloned.1.call-done), kind=kOutput, calls=%fused_computation.8 | convolution fusion | flops 2824077312 | bytes 11862016 | tf_op jit(solution)/shard_map/dot_general | solution.py:20
  438.9 36.8 %reduce-scatter.5.cloned.1.call-done = f32[24,2048]{1,0:T(8,128)} async-done(((f32[768,2048]{1,0:T(8,128)}), f32[24,2048]{1,0:T(8,128)}) %reduce-scatter.5.cloned.1.call-update) | async-done | bytes 196624 | tf_op jit(solution)/shard_map/reduce_scatter | solution.py:60
  475.7 1.6 convert_element_type.79
  477.3 88.1 %reduce-scatter.3.cloned.1.call-done = f32[24,2048]{1,0:T(8,128)} async-done(((f32[768,2048]{1,0:T(8,128)}), f32[24,2048]{1,0:T(8,128)}) %reduce-scatter.3.cloned.1.call-update) | async-done | bytes 196624 | tf_op jit(solution)/shard_map/reduce_scatter | solution.py:47
  565.4 1.6 convert_element_type.76
  (1 shorter events, 0.0 us)
Async XLA Ops:
  7.2 50.8 %all-gather.5.cloned.1.call-start = ((), (), s32[]{:S(2)}) async-start(), calls=%async_computation.2 | async-start | bytes 3244032 | tf_op jit(solution)/shard_map/all_gather | solution.py:40
  7.9 96.8 %all-gather.7.cloned.1.call-start = ((), (), s32[]{:S(2)}) async-start(), calls=%async_computation.4 | async-start | bytes 3244032 | tf_op jit(solution)/shard_map/all_gather | solution.py:53
  8.6 295.2 %all-gather.9.cloned.1.call-start = ((), (), s32[]{:S(2)}) async-start(), calls=%async_computation.7 | async-start | bytes 27525120 | tf_op jit(solution)/shard_map/all_gather | solution.py:43
  70.4 0.7 copy-start.3
  70.4 305.5 %all-reduce.2.cloned.1.call-start = ((), (), s32[]{:S(2)}) async-start(), calls=%async_computation.5 | async-start | bytes 5505024 | tf_op jit(solution)/shard_map/psum | solution.py:55
  112.3 363.4 %reduce-scatter.5.cloned.1.call-start = ((), (), s32[]{:S(2)}) async-start(), calls=%async_computation.6 | async-start | bytes 6488064 | tf_op jit(solution)/shard_map/reduce_scatter | solution.py:60
  375.9 4.5 copy-start.1
  380.2 3.7 copy-start.2
  380.3 3.5 copy-start
  389.3 176.1 %reduce-scatter.3.cloned.1.call-start = ((), (), s32[]{:S(2)}) async-start(), calls=%async_computation.3 | async-start | bytes 6488064 | tf_op jit(solution)/shard_map/reduce_scatter | solution.py:47
Sparse Core Ops, SparseCore 0:
  10.3 47.6 all-gather.4
  60.2 44.4 all-gather.6
  106.4 197.3 all-gather.8
  306.0 69.7 all-reduce.1
  389.4 86.1 reduce-scatter.4
  479.7 85.6 reduce-scatter.2
